TPU v7x, 256 devices: a whole 4x4x8 slice. The times are simulated.
256 devices in a mesh: dp: 8 (over x, core), cut: 32 (over y, z).
Axes of the slice: x: 4, y: 4, z: 8, core: 2. Of those that a mesh axis runs over, the one named last changes fastest.
Arguments:
- node_feat: bfloat16 [128, 262144], P(None, ('dp', 'cut')), parts along dimension 1, may hold values from -6 to 6
- edge_feat: bfloat16 [128, 1048576], P(None, ('dp', 'cut')), parts along dimension 1, may hold values from -6 to 6
- route: int32 [256, 32, 128], P(('dp', 'cut')), parts along dimension 0, may hold values from 0 to 1023, as said below
- block_tile: int32 [8192, 2], P(('dp', 'cut')), parts along dimension 0, may hold values from 0 to 39
- block_offset: int32 [8192, 2, 128], P(('dp', 'cut')), parts along dimension 0, may hold values from 0 to 127
- block_count: int32 [8192], P(('dp', 'cut')), parts along dimension 0, may hold values from 1 to 128, as said below
- w_edge1: bfloat16 [128, 384], replicated, may hold values from -0.3125 to 0.3125
- bias_edge1: float32 [128], replicated, may hold values from -3 to 3
- w_edge2: bfloat16 [128, 128], replicated, may hold values from -0.5 to 0.5
- gain_edge: float32 [128], replicated, may hold values from 0.1 to 1.9
- shift_edge: float32 [128], replicated, may hold values from -3 to 3
- w_node1: bfloat16 [128, 256], replicated, may hold values from -0.375 to 0.375
- bias_node1: float32 [128], replicated, may hold values from -3 to 3
- w_node2: bfloat16 [128, 128], replicated, may hold values from -0.5 to 0.5
- gain_node: float32 [128], replicated, may hold values from 0.1 to 1.9
- shift_node: float32 [128], replicated, may hold values from -3 to 3
- node_cot: bfloat16 [128, 262144], P(None, ('dp', 'cut')), parts along dimension 1, may hold values from -6 to 6
Outputs:
- node_out: bfloat16 [128, 262144], P(None, ('dp', 'cut')), parts along dimension 1
- node_grad: float32 [128, 262144], P(None, ('dp', 'cut')), parts along dimension 1
- edge_grad: bfloat16 [128, 1048576], P(None, ('dp', 'cut')), parts along dimension 1
- param_grad: float32 [923648], P('dp'), parts along dimension 0
There are 8 independent parts, one for each index of `dp`. A program takes and returns all parts, laid end to end along the dimension named above; an argument that names none is the same for every part. Nothing has to cross between parts.
Inputs may be any that keep to these rules, and one draw needn't show every extreme that they name: route[c, p, :] holds 128 distinct master rows of partition p. `block_count`: the first block of each partition is full.
All inputs are finite; a program needn't handle non-finite values.
Results may differ from a plain program's by a relative error of at most 0.024.
Values may be sent and summed in bfloat16 or wider, within the bound.
No kernel may reach another device: no remote copies, remote signals or barrier semaphores. Data moves between devices by JAX's collectives and lax.ppermute only.
A program may use at most 128 MiB of HBM per device.

v0:
```python
import math
import jax
import jax.numpy as jnp
from jax import lax
from jax.sharding import PartitionSpec as P


def silu_slope(values):
    sigmoid_val = jax.nn.sigmoid(values)
    return sigmoid_val * (1.0 + values * (1.0 - sigmoid_val))


def layer_norm(values):
    centred = values - jnp.mean(values, axis=0, keepdims=True)
    inverse = lax.rsqrt(jnp.mean(centred * centred, axis=0, keepdims=True) + 1e-05)
    return (centred * inverse, inverse)


def norm_back(upstream, normed, inverse, gain_vec):
    scaled = upstream * gain_vec[:, None]
    return inverse * (
        scaled
        - jnp.mean(scaled, axis=0, keepdims=True)
        - normed * jnp.mean(scaled * normed, axis=0, keepdims=True)
    )


def row_contract(left, right):
    return lax.dot_general(
        left, right, (((1,), (1,)), ((), ())), preferred_element_type=jnp.float32
    )


def lead_contract(weight, values):
    return lax.dot_general(
        weight, values, (((0,), (0,)), ((), ())), preferred_element_type=jnp.float32
    )


def per_device(
    node_feat,
    edge_feat,
    route,
    block_tile,
    block_offset,
    block_count,
    w_edge1,
    bias_edge1,
    w_edge2,
    gain_edge,
    shift_edge,
    w_node1,
    bias_node1,
    w_node2,
    gain_node,
    shift_node,
    node_cot,
):
    latent = node_feat.shape[0]
    masters = node_feat.shape[1]
    peer_count = lax.axis_size("cut")
    total_nodes = masters * peer_count
    total_edges = edge_feat.shape[1] * peer_count
    mirror_index = lax.all_to_all(route[0], "cut", split_axis=0, concat_axis=0, tiled=True).reshape(
        -1
    )

    def fetch_mirrors(master_part):
        outgoing = jnp.take(master_part, mirror_index, axis=1)
        result = lax.all_to_all(outgoing, "cut", split_axis=1, concat_axis=1, tiled=True)
        return result

    def reduce_mirrors(master_part, mirror_part):
        returned = lax.all_to_all(
            mirror_part.astype(jnp.bfloat16), "cut", split_axis=1, concat_axis=1, tiled=True
        ).astype(mirror_part.dtype)
        result = master_part.at[:, mirror_index].add(returned)
        return result

    columns = 128 * block_tile[:, :, None] + block_offset
    send_cols = columns[:, 0, :].reshape(-1)
    recv_cols = columns[:, 1, :].reshape(-1)
    live_mask = (
        (jnp.arange(block_offset.shape[2], dtype=jnp.int32)[None, :] < block_count[:, None])
        .reshape(-1)
        .astype(jnp.float32)
    )
    node_table = jnp.concatenate([node_feat, fetch_mirrors(node_feat)], axis=1)
    local_width = node_table.shape[1]
    stacked = jnp.concatenate(
        [
            edge_feat,
            jnp.take(node_table, send_cols, axis=1),
            jnp.take(node_table, recv_cols, axis=1),
        ],
        axis=0,
    )
    edge_pre = jnp.dot(w_edge1, stacked, preferred_element_type=jnp.float32) + bias_edge1[:, None]
    edge_hidden = jax.nn.silu(edge_pre).astype(jnp.bfloat16)
    edge_post = jnp.dot(w_edge2, edge_hidden, preferred_element_type=jnp.float32)
    edge_normed, edge_inv = layer_norm(edge_post)
    message = (gain_edge[:, None] * edge_normed + shift_edge[:, None]) * live_mask[None, :]
    local_sums = jnp.zeros((latent, local_width), jnp.float32).at[:, recv_cols].add(message)
    aggregate = reduce_mirrors(local_sums[:, :masters], local_sums[:, masters:])
    agg_low = aggregate.astype(jnp.bfloat16)
    node_input = jnp.concatenate([node_feat, agg_low], axis=0)
    node_pre = (
        jnp.dot(w_node1, node_input, preferred_element_type=jnp.float32) + bias_node1[:, None]
    )
    node_hidden = jax.nn.silu(node_pre).astype(jnp.bfloat16)
    node_post = jnp.dot(w_node2, node_hidden, preferred_element_type=jnp.float32)
    node_normed, node_inv = layer_norm(node_post)
    node_out = (
        node_feat.astype(jnp.float32) + gain_node[:, None] * node_normed + shift_node[:, None]
    ).astype(jnp.bfloat16)
    upstream = node_cot.astype(jnp.float32)
    grad_gain_node = jnp.sum(upstream * node_normed, axis=1)
    grad_shift_node = jnp.sum(upstream, axis=1)
    grad_node_post = norm_back(upstream, node_normed, node_inv, gain_node).astype(jnp.bfloat16)
    grad_w_node2 = row_contract(grad_node_post, node_hidden)
    grad_node_full = lead_contract(w_node2, grad_node_post) * silu_slope(node_pre)
    grad_node_pre = grad_node_full.astype(jnp.bfloat16)
    grad_w_node1 = row_contract(grad_node_pre, node_input)
    grad_bias_node1 = jnp.sum(grad_node_full, axis=1)
    node_direct = lead_contract(w_node1[:, :latent], grad_node_pre)
    grad_agg = lead_contract(w_node1[:, latent:], grad_node_pre).astype(jnp.bfloat16)
    node_vec = jnp.concatenate(
        [
            grad_w_node1.reshape(-1),
            grad_bias_node1,
            grad_w_node2.reshape(-1),
            grad_gain_node,
            grad_shift_node,
        ]
    )
    agg_table = jnp.concatenate([grad_agg, fetch_mirrors(grad_agg)], axis=1)
    grad_message = jnp.take(agg_table, recv_cols, axis=1).astype(jnp.float32) * live_mask[None, :]
    grad_gain_edge = jnp.sum(grad_message * edge_normed, axis=1)
    grad_shift_edge = jnp.sum(grad_message, axis=1)
    grad_edge_post = norm_back(grad_message, edge_normed, edge_inv, gain_edge).astype(jnp.bfloat16)
    grad_w_edge2 = row_contract(grad_edge_post, edge_hidden)
    grad_edge_full = lead_contract(w_edge2, grad_edge_post) * silu_slope(edge_pre)
    grad_edge_pre = grad_edge_full.astype(jnp.bfloat16)
    grad_w_edge1 = row_contract(grad_edge_pre, stacked)
    grad_bias_edge1 = jnp.sum(grad_edge_full, axis=1)
    edge_grad = lead_contract(w_edge1[:, :latent], grad_edge_pre).astype(jnp.bfloat16)
    grad_send = lead_contract(w_edge1[:, latent : 2 * latent], grad_edge_pre)
    grad_recv = lead_contract(w_edge1[:, 2 * latent :], grad_edge_pre)
    grad_table = (
        jnp.zeros((latent, local_width), jnp.float32)
        .at[:, send_cols]
        .add(grad_send)
        .at[:, recv_cols]
        .add(grad_recv)
    )
    node_grad = (
        upstream + node_direct + reduce_mirrors(grad_table[:, :masters], grad_table[:, masters:])
    )
    edge_vec = jnp.concatenate(
        [
            grad_w_edge1.reshape(-1),
            grad_bias_edge1,
            grad_w_edge2.reshape(-1),
            grad_gain_edge,
            grad_shift_edge,
        ]
    )
    summed = lax.psum(jnp.concatenate([edge_vec, node_vec]).astype(jnp.bfloat16), "cut").astype(
        jnp.float32
    )
    edge_summed = summed[: edge_vec.shape[0]]
    node_summed = summed[edge_vec.shape[0] :]
    param_grad = jnp.concatenate(
        [edge_summed / math.sqrt(total_edges), node_summed / math.sqrt(total_nodes)]
    )
    return (node_out, node_grad, edge_grad, param_grad)


def solution(mesh):
    in_specs = (
        P(None, ("dp", "cut")),
        P(None, ("dp", "cut")),
        P(("dp", "cut"), None, None),
        P(("dp", "cut"), None),
        P(("dp", "cut"), None, None),
        P(("dp", "cut")),
        P(),
        P(),
        P(),
        P(),
        P(),
        P(),
        P(),
        P(),
        P(),
        P(),
        P(None, ("dp", "cut")),
    )
    out_specs = (P(None, ("dp", "cut")), P(None, ("dp", "cut")), P(None, ("dp", "cut")), P("dp"))
    return jax.shard_map(
        per_device, mesh=mesh, in_specs=in_specs, out_specs=out_specs, check_vma=False
    )
```

profile of v0, /device:TPU:2, one launch (start us, length us, event | category | flops | bytes accessed | tf_op | source)
XLA Modules:
  0.0 506.6 jit_solution(10482661762203878273)
XLA Ops:
  7.2 11.5 %all-to-all-start = ((s32[32,1,128]{2,1,0:T(1,128)}), s32[32,1,128]{2,1,0:T(1,128)S(1)}, u32[]{:S(2)}, u32[]{:S(2)}) async-start(s32[32,1,128]{2,1,0:T(1,128)} %bitcast.144), calls=%async_computation | async-start | bytes 32768 | tf_op jit(solution)/shard_map/all_to_all | solution.py:64
  21.4 7.0 %all-to-all-done = s32[32,1,128]{2,1,0:T(1,128)S(1)} async-done(((s32[32,1,128]{2,1,0:T(1,128)}), s32[32,1,128]{2,1,0:T(1,128)S(1)}, u32[]{:S(2)}, u32[]{:S(2)}) %all-to-all-start) | async-done | bytes 16416 | tf_op jit(solution)/shard_map/all_to_all | solution.py:64
  28.4 12.1 %gather_fusion = bf16[4096,128]{1,0:T(8,128)(2,1)S(1)} fusion(bf16[128,1024]{0,1:T(8,128)(2,1)S(1)} %copy.38, s32[4096]{0:T(1024)S(1)} %fusion.48), kind=kCustom, calls=%fused_computation.clone | custom fusion | bytes 2113536 | tf_op jit(solution)/shard_map/jit(_take)/gather | solution.py:69
  40.6 2.9 broadcast_select_fusion.1
  43.5 3.9 all-to-all-start.1
  49.6 25.4 %all-to-all-done.1 = bf16[128,32,128]{0,2,1:T(8,128)(2,1)S(1)} async-done(((bf16[128,32,128]{0,2,1:T(8,128)(2,1)}), bf16[128,32,128]{0,2,1:T(8,128)(2,1)S(1)}, u32[]{:S(2)}, u32[]{:S(2)}) %all-to-all-start.1) | async-done | bytes 1048608 | tf_op jit(solution)/shard_map/all_to_all | solution.py:70
  75.1 12.1 %gather_fusion.1 = bf16[4096,128]{1,0:T(8,128)(2,1)S(1)} fusion(bf16[128,5120]{0,1:T(8,128)(2,1)S(1)} %pad_maximum_fusion.1, s32[4096]{0:T(1024)S(1)} %fusion.49), kind=kCustom, calls=%fused_computation.1.clone | custom fusion | bytes 2113536 | tf_op jit(solution)/shard_map/jit(_take)/gather | solution.py:93
  87.2 15.0 %gather_fusion.2 = bf16[4096,128]{1,0:T(8,128)(2,1)} fusion(bf16[128,5120]{0,1:T(8,128)(2,1)S(1)} %pad_maximum_fusion.1, s32[4096]{0:T(1024)S(1)} %fusion.50), kind=kCustom, calls=%fused_computation.3.clone | custom fusion | bytes 2113536 | tf_op jit(solution)/shard_map/jit(_take)/gather | solution.py:94
  102.3 3.1 select_bitcast_fusion
  111.8 23.3 %scatter_custom_fusion = f32[128,5120]{0,1:T(8,128)S(1)} fusion(s32[4096]{0:T(1024)S(1)} %bitcast.142, f32[4096,128]{1,0:T(8,128)} %copy.37, f32[]{:T(128)} %constant.26.clone.1), kind=kCustom, calls=%fused_computation.47 | custom fusion | flops 524288 | bytes 2621952 | tf_op jit(solution)/shard_map/scatter-add | solution.py:103
  136.2 5.1 %all-to-all-start.2 = ((bf16[128,32,128]{0,2,1:T(8,128)(2,1)}), bf16[128,32,128]{0,2,1:T(8,128)(2,1)}, u32[]{:S(2)}, u32[]{:S(2)}) async-start(bf16[128,32,128]{0,2,1:T(8,128)(2,1)} %bitcast.134), calls=%async_computation.2 | async-start | bytes 2097152 | tf_op jit(solution)/shard_map/all_to_all | solution.py:74
  141.4 27.5 %all-to-all-done.2 = bf16[128,32,128]{0,2,1:T(8,128)(2,1)} async-done(((bf16[128,32,128]{0,2,1:T(8,128)(2,1)}), bf16[128,32,128]{0,2,1:T(8,128)(2,1)}, u32[]{:S(2)}, u32[]{:S(2)}) %all-to-all-start.2) | async-done | bytes 1048608 | tf_op jit(solution)/shard_map/all_to_all | solution.py:74
  168.9 23.1 %scatter_custom_fusion.1 = f32[128,1024]{0,1:T(8,128)S(1)} fusion(f32[128,1024]{0,1:T(8,128)S(1)} %slice.66, s32[4096]{0:T(1024)S(1)} %bitcast.145, bf16[128,4096]{0,1:T(8,128)(2,1)} %bitcast.39), kind=kCustom, calls=%fused_computation.22 | custom fusion | flops 1048576 | bytes 1572864 | tf_op jit(solution)/shard_map/scatter-add | solution.py:77
  196.7 12.1 %gather_fusion.3 = bf16[4096,128]{1,0:T(8,128)(2,1)S(1)} fusion(bf16[128,1024]{0,1:T(8,128)(2,1)S(1)} %fusion.25, s32[4096]{0:T(1024)S(1)} %fusion.48), kind=kCustom, calls=%fused_computation.2.clone | custom fusion | bytes 2113536 | tf_op jit(solution)/shard_map/jit(_take)/gather | solution.py:69
  208.8 2.9 broadcast_select_fusion
  211.7 5.0 all-to-all-start.3
  218.6 25.7 %all-to-all-done.3 = bf16[128,32,128]{0,2,1:T(8,128)(2,1)S(1)} async-done(((bf16[128,32,128]{0,2,1:T(8,128)(2,1)}), bf16[128,32,128]{0,2,1:T(8,128)(2,1)S(1)}, u32[]{:S(2)}, u32[]{:S(2)}) %all-to-all-start.3) | async-done | bytes 1048608 | tf_op jit(solution)/shard_map/all_to_all | solution.py:70
  244.4 15.0 %gather_fusion.4 = bf16[4096,128]{1,0:T(8,128)(2,1)} fusion(bf16[128,5120]{0,1:T(8,128)(2,1)S(1)} %pad_maximum_fusion.2, s32[4096]{0:T(1024)S(1)} %copy-done.18), kind=kCustom, calls=%fused_computation.4.clone | custom fusion | bytes 2113536 | tf_op jit(solution)/shard_map/jit(_take)/gather | solution.py:137
  261.4 2.5 fusion.12
  274.8 23.3 %scatter_custom_fusion.2 = f32[128,5120]{0,1:T(8,128)S(1)} fusion(s32[4096]{0:T(1024)} %bitcast.147, f32[4096,128]{1,0:T(8,128)} %fusion.44, f32[]{:T(128)} %constant.26.clone.1), kind=kCustom, calls=%fused_computation.45 | custom fusion | flops 524288 | bytes 2621952 | tf_op jit(solution)/shard_map/scatter-add | solution.py:152
  298.1 23.8 %scatter_fusion = f32[128,5120]{0,1:T(8,128)S(1)} fusion(f32[128,5120]{0,1:T(8,128)S(1)} %scatter_custom_fusion.2, s32[4096]{0:T(1024)S(1)} %bitcast.143, f32[4096,128]{1,0:T(8,128)} %fusion.42), kind=kCustom, calls=%fused_computation.8 | custom fusion | flops 524288 | bytes 6307840 | tf_op jit(solution)/shard_map/scatter-add | solution.py:154
  332.8 5.0 all-to-all-start.4
  337.8 136.4 %all-reduce.2.cloned.1.call-done = bf16[115456]{0:T(1024)(128)(2,1)} async-done(((bf16[115456]{0:T(1024)(128)(2,1)}), bf16[115456]{0:T(1024)(128)(2,1)}) %all-reduce.2.cloned.1.call-update) | async-done | bytes 230928 | tf_op jit(solution)/shard_map/psum | solution.py:168
  476.1 22.7 %scatter_custom_fusion.4 = f32[128,1024]{0,1:T(8,128)S(1)} fusion(f32[128,1024]{0,1:T(8,128)S(1)} %copy.42, s32[4096]{0:T(1024)} %bitcast.146, bf16[128,4096]{0,1:T(8,128)(2,1)S(1)} %bitcast.132), kind=kCustom, calls=%fused_computation.20 | custom fusion | flops 1048576 | bytes 1572864 | tf_op jit(solution)/shard_map/scatter-add | solution.py:77
  (161 shorter events, 45.3 us)
Async XLA Ops:
  7.2 100.6 %copy-start = (bf16[128,128]{1,0:T(8,128)(2,1)S(1)}, bf16[128,128]{1,0:T(8,128)(2,1)}, u32[]{:S(2)}) copy-start(bf16[128,128]{1,0:T(8,128)(2,1)} %param.29) | copy-start | bytes 98308
  7.2 21.2 %all-to-all-start = ((s32[32,1,128]{2,1,0:T(1,128)}), s32[32,1,128]{2,1,0:T(1,128)S(1)}, u32[]{:S(2)}, u32[]{:S(2)}) async-start(s32[32,1,128]{2,1,0:T(1,128)} %bitcast.144), calls=%async_computation | async-start | bytes 32768 | tf_op jit(solution)/shard_map/all_to_all | solution.py:64
  40.6 6.8 %copy-start.38 = (s32[32]{0:T(128)S(1)}, s32[32]{0:T(128)}, u32[]{:S(2)}) copy-start(s32[32]{0:T(128)} %param.26) | copy-start | bytes 388
  40.6 6.9 %copy-start.8 = (bf16[128,4096]{1,0:T(8,128)(2,1)S(1)}, bf16[128,4096]{1,0:T(8,128)(2,1)}, u32[]{:S(2)}) copy-start(bf16[128,4096]{1,0:T(8,128)(2,1)} %param.22) | copy-start | bytes 3145732
  43.5 31.5 %all-to-all-start.1 = ((bf16[128,32,128]{0,2,1:T(8,128)(2,1)}), bf16[128,32,128]{0,2,1:T(8,128)(2,1)S(1)}, u32[]{:S(2)}, u32[]{:S(2)}) async-start(bf16[128,32,128]{0,2,1:T(8,128)(2,1)} %bitcast.6), calls=%async_computation.1 | async-start | bytes 2097152 | tf_op jit(solution)/shard_map/all_to_all | solution.py:70
  48.9 53.4 %copy-start.25 = (pred[4096]{0:T(1024)(128)(4,1)}, pred[4096]{0:T(1024)(128)(4,1)S(1)}, u32[]{:S(2)}) copy-start(pred[4096]{0:T(1024)(128)(4,1)S(1)} %compare_and_fusion) | copy-start | bytes 12292
  48.9 38.3 %copy-start.17 = (s32[4096]{0:T(1024)}, s32[4096]{0:T(1024)S(1)}, u32[]{:S(2)}) copy-start(s32[4096]{0:T(1024)S(1)} %fusion.50) | copy-start | bytes 49156
  49.6 62.2 %copy-start.21 = (s32[4096,1]{0,1:T(1,128)}, s32[4096,1]{0,1:T(1,128)S(1)}, u32[]{:S(2)}) copy-start(s32[4096,1]{0,1:T(1,128)S(1)} %get-tuple-element.26) | copy-start | bytes 49156
  102.3 3.1 copy-start.39
  136.2 32.8 %all-to-all-start.2 = ((bf16[128,32,128]{0,2,1:T(8,128)(2,1)}), bf16[128,32,128]{0,2,1:T(8,128)(2,1)}, u32[]{:S(2)}, u32[]{:S(2)}) async-start(bf16[128,32,128]{0,2,1:T(8,128)(2,1)} %bitcast.134), calls=%async_computation.2 | async-start | bytes 2097152 | tf_op jit(solution)/shard_map/all_to_all | solution.py:74
  141.3 50.8 %copy-start.40 = (f32[128]{0:T(128)S(1)}, f32[128]{0:T(128)}, u32[]{:S(2)}) copy-start(f32[128]{0:T(128)} %param.33) | copy-start | bytes 1540
  141.4 52.1 %copy-start.28 = (s32[4096,1]{0,1:T(1,128)}, s32[4096,1]{0,1:T(1,128)S(1)}, u32[]{:S(2)}) copy-start(s32[4096,1]{0,1:T(1,128)S(1)} %compare_select_fusion.1) | copy-start | bytes 49156
  196.5 21.0 %copy-start.6 = (bf16[128,1024]{0,1:T(8,128)(2,1)}, bf16[128,1024]{0,1:T(8,128)(2,1)S(1)}, u32[]{:S(2)}) copy-start(bf16[128,1024]{0,1:T(8,128)(2,1)S(1)} %get-tuple-element.39) | copy-start | bytes 786436
  211.7 32.6 %all-to-all-start.3 = ((bf16[128,32,128]{0,2,1:T(8,128)(2,1)}), bf16[128,32,128]{0,2,1:T(8,128)(2,1)S(1)}, u32[]{:S(2)}, u32[]{:S(2)}) async-start(bf16[128,32,128]{0,2,1:T(8,128)(2,1)} %bitcast.28), calls=%async_computation.3 | async-start | bytes 2097152 | tf_op jit(solution)/shard_map/all_to_all | solution.py:70
  216.7 257.5 %all-reduce.2.cloned.1.call-start = ((), (), s32[]{:S(2)}) async-start(), calls=%async_computation.5 | async-start | bytes 462848 | tf_op jit(solution)/shard_map/psum | solution.py:168
  217.4 27.0 %copy-start.18 = (s32[4096]{0:T(1024)S(1)}, s32[4096]{0:T(1024)}, u32[]{:S(2)}) copy-start(s32[4096]{0:T(1024)} %copy-done.17) | copy-start | bytes 49156
  274.8 23.3 %copy-start.22 = (s32[4096,1]{0,1:T(1,128)S(1)}, s32[4096,1]{0,1:T(1,128)}, u32[]{:S(2)}) copy-start(s32[4096,1]{0,1:T(1,128)} %copy-done.21) | copy-start | bytes 49156
  322.0 3.5 copy-start.35
  322.0 3.8 copy-start.34
  322.0 6.7 %copy-start.32 = (bf16[128]{0:T(256)(128)(2,1)S(1)}, bf16[128]{0:T(256)(128)(2,1)}, u32[]{:S(2)}) copy-start(bf16[128]{0:T(256)(128)(2,1)} %get-tuple-element.18) | copy-start | bytes 772
  322.0 7.0 %copy-start.33 = (bf16[128]{0:T(256)(128)(2,1)S(1)}, bf16[128]{0:T(256)(128)(2,1)}, u32[]{:S(2)}) copy-start(bf16[128]{0:T(256)(128)(2,1)} %reduce.4) | copy-start | bytes 772
  323.1 9.2 %copy-start.7 = (bf16[128,1024]{0,1:T(8,128)(2,1)S(1)}, bf16[128,1024]{0,1:T(8,128)(2,1)}, u32[]{:S(2)}) copy-start(bf16[128,1024]{0,1:T(8,128)(2,1)} %copy-done.6) | copy-start | bytes 786436
  323.1 9.2 %copy-start.24 = (bf16[128,256]{1,0:T(8,128)(2,1)S(1)}, bf16[128,256]{1,0:T(8,128)(2,1)}, u32[]{:S(2)}) copy-start(bf16[128,256]{1,0:T(8,128)(2,1)} %param.32) | copy-start | bytes 196612
  332.8 143.2 %all-to-all-start.4 = ((bf16[128,32,128]{0,2,1:T(8,128)(2,1)}), bf16[128,32,128]{0,2,1:T(8,128)(2,1)S(1)}, u32[]{:S(2)}, u32[]{:S(2)}) async-start(bf16[128,32,128]{0,2,1:T(8,128)(2,1)} %bitcast.32), calls=%async_computation.4 | async-start | bytes 2097152 | tf_op jit(solution)/shard_map/all_to_all | solution.py:74
  (24 other events, 44.7 us)
Sparse Core Ops, SparseCore 0:
  330.0 144.1 all-reduce.1
where the time goes:
time: 508 us; the launch traced here: 507 us
  waiting for transfers between devices  222 us (44%)
  other arithmetic  136 us (27%)
  local copies, waits for them, and re-layouts  88.5 us (17%)
  starting transfers between devices  30.5 us (6%)
  matrix products  14.8 us (3%)
  between operations  14.8 us (3%)
    psum x1, waiting for transfers between devices, per_device(): lax.psum(jnp.concatenate([edge_vec, node_vec]).astype(jnp.bfloat16), 'cut')  136 us
    all_to_all x2, waiting for transfers between devices, fetch_mirrors(): lax.all_to_all(outgoing, 'cut', split_axis=1, concat_axis=1, tiled=True)  51.1 us
    scatter-add x2, other arithmetic, per_device(): grad_table = jnp.zeros((latent, local_width), jnp.float32).at[:, send_col...  47.1 us
    scatter-add x2, other arithmetic, reduce_mirrors(): result = master_part.at[:, mirror_index].add(returned)  45.9 us
    all_to_all x2, waiting for transfers between devices, reduce_mirrors(): lax.all_to_all(mirror_part.astype(jnp.bfloat16), 'cut', split_axis=1, con...  27.5 us
    gather x2, local copies, waits for them, and re-layouts, fetch_mirrors(): outgoing = jnp.take(master_part, mirror_index, axis=1)  24.3 us
    scatter-add x1, other arithmetic, per_device(): jnp.zeros((latent, local_width), jnp.float32).at[:, recv_cols].add(message)  23.3 us
    gather x2, local copies, waits for them, and re-layouts, per_device(): jnp.take(agg_table, recv_cols, axis=1).astype(jnp.float32)  16.7 us
  transfers between devices with their start and end apart: 6, of which 5 were waited for; matrix products, arithmetic and copies ran while one was open for 2% of the time, Pallas kernels for 0%

commit v1 on v0

--- a/solution.py
+++ b/solution.py
@@ -3,6 +3,11 @@
 import jax.numpy as jnp
 from jax import lax
 from jax.sharding import PartitionSpec as P
+
+
+def summed_here(block, mesh_axis):
+    parts = lax.all_gather(block, mesh_axis)
+    return jnp.sum(parts, axis=0)
 
 
 def silu_slope(values):
@@ -165,7 +170,7 @@
             grad_shift_edge,
         ]
     )
-    summed = lax.psum(jnp.concatenate([edge_vec, node_vec]).astype(jnp.bfloat16), "cut").astype(
+    summed = summed_here(jnp.concatenate([edge_vec, node_vec]).astype(jnp.bfloat16), "cut").astype(
         jnp.float32
     )
     edge_summed = summed[: edge_vec.shape[0]]

time: 508 us -> 447 us (0.88)
  waiting for transfers between devices: 222 us -> 146 us
  other arithmetic: 136 us -> 155 us
    psum x1 -> x0, waiting for transfers between devices: 136 us -> none  [per_device(): lax.psum(jnp.concatenate([edge_vec, node_vec]).astype(jnp.bfloat16), 'cut')]
    all_to_all x2, waiting for transfers between devices: 27.5 us -> 62 us  [reduce_mirrors(): lax.all_to_all(mirror_part.astype(jnp.bfloat16), 'cut', split_axis=1, con...]
    all_gather x0 -> x1, waiting for transfers between devices: none -> 24.8 us  [summed_here(): parts = lax.all_gather(block, mesh_axis)]
    reduce_sum x0 -> x1, other arithmetic: none -> 20.8 us  [summed_here(): return jnp.sum(parts, axis=0)]
    unnamed x99 -> x114, local copies, waits for them, and re-layouts: 14.8 us -> 11.1 us
  transfers between devices with their start and end apart: 6 -> 6, of which waited for: 5 -> 6; matrix products, arithmetic and copies ran while one was open for 2% -> 20% of each run, Pallas kernels for 0% -> 0%
where the time goes in v1:
time: 447 us; the launch traced here: 446 us
  other arithmetic  155 us (35%)
  waiting for transfers between devices  146 us (33%)
  local copies, waits for them, and re-layouts  83.6 us (19%)
  starting transfers between devices  30.9 us (7%)
  matrix products  15.4 us (3%)
  between operations  14.9 us (3%)
    all_to_all x2, waiting for transfers between devices, reduce_mirrors(): lax.all_to_all(mirror_part.astype(jnp.bfloat16), 'cut', split_axis=1, con...  62 us
    all_to_all x2, waiting for transfers between devices, fetch_mirrors(): lax.all_to_all(outgoing, 'cut', split_axis=1, concat_axis=1, tiled=True)  51 us
    scatter-add x2, other arithmetic, per_device(): grad_table = jnp.zeros((latent, local_width), jnp.float32).at[:, send_col...  47.1 us
    scatter-add x2, other arithmetic, reduce_mirrors(): result = master_part.at[:, mirror_index].add(returned)  46.1 us
    all_gather x1, waiting for transfers between devices, summed_here(): parts = lax.all_gather(block, mesh_axis)  24.8 us
    gather x2, local copies, waits for them, and re-layouts, fetch_mirrors(): outgoing = jnp.take(master_part, mirror_index, axis=1)  24.3 us
    scatter-add x1, other arithmetic, per_device(): jnp.zeros((latent, local_width), jnp.float32).at[:, recv_cols].add(message)  23.3 us
    reduce_sum x1, other arithmetic, summed_here(): return jnp.sum(parts, axis=0)  20.8 us
  transfers between devices with their start and end apart: 6, of which 6 were waited for; matrix products, arithmetic and copies ran while one was open for 20% of the time, Pallas kernels for 0%

profile of v1, /device:TPU:2, one launch (start us, length us, event | category | flops | bytes accessed | tf_op | source)
XLA Modules:
  0.0 445.6 jit_solution(6015282421839211149)
XLA Ops:
  7.2 11.5 %all-to-all-start = ((s32[32,1,128]{2,1,0:T(1,128)}), s32[32,1,128]{2,1,0:T(1,128)S(1)}, u32[]{:S(2)}, u32[]{:S(2)}) async-start(s32[32,1,128]{2,1,0:T(1,128)} %bitcast.172), calls=%async_computation | async-start | bytes 32768 | tf_op jit(solution)/shard_map/all_to_all | solution.py:69
  20.5 7.9 %all-to-all-done = s32[32,1,128]{2,1,0:T(1,128)S(1)} async-done(((s32[32,1,128]{2,1,0:T(1,128)}), s32[32,1,128]{2,1,0:T(1,128)S(1)}, u32[]{:S(2)}, u32[]{:S(2)}) %all-to-all-start) | async-done | bytes 16416 | tf_op jit(solution)/shard_map/all_to_all | solution.py:69
  28.4 12.1 %gather_fusion = bf16[4096,128]{1,0:T(8,128)(2,1)S(1)} fusion(bf16[128,1024]{0,1:T(8,128)(2,1)S(1)} %copy.38, s32[4096]{0:T(1024)S(1)} %fusion.49), kind=kCustom, calls=%fused_computation.clone | custom fusion | bytes 2113536 | tf_op jit(solution)/shard_map/jit(_take)/gather | solution.py:74
  40.6 2.9 broadcast_select_fusion.1
  43.5 4.1 all-to-all-start.1
  49.8 25.3 %all-to-all-done.1 = bf16[128,32,128]{0,2,1:T(8,128)(2,1)S(1)} async-done(((bf16[128,32,128]{0,2,1:T(8,128)(2,1)}), bf16[128,32,128]{0,2,1:T(8,128)(2,1)S(1)}, u32[]{:S(2)}, u32[]{:S(2)}) %all-to-all-start.1) | async-done | bytes 1048608 | tf_op jit(solution)/shard_map/all_to_all | solution.py:75
  75.2 12.1 %gather_fusion.1 = bf16[4096,128]{1,0:T(8,128)(2,1)S(1)} fusion(bf16[128,5120]{0,1:T(8,128)(2,1)S(1)} %pad_maximum_fusion.1, s32[4096]{0:T(1024)S(1)} %get-tuple-element.40), kind=kCustom, calls=%fused_computation.1.clone | custom fusion | bytes 2113536 | tf_op jit(solution)/shard_map/jit(_take)/gather | solution.py:98
  87.3 15.0 %gather_fusion.2 = bf16[4096,128]{1,0:T(8,128)(2,1)} fusion(bf16[128,5120]{0,1:T(8,128)(2,1)S(1)} %pad_maximum_fusion.1, s32[4096]{0:T(1024)S(1)} %get-tuple-element.41), kind=kCustom, calls=%fused_computation.3.clone | custom fusion | bytes 2113536 | tf_op jit(solution)/shard_map/jit(_take)/gather | solution.py:99
  113.2 23.3 %scatter_custom_fusion = f32[128,5120]{0,1:T(8,128)S(1)} fusion(s32[4096]{0:T(1024)S(1)} %bitcast.170, f32[4096,128]{1,0:T(8,128)} %copy.37, f32[]{:T(128)} %constant.27.clone.1), kind=kCustom, calls=%fused_computation.47 | custom fusion | flops 524288 | bytes 2621952 | tf_op jit(solution)/shard_map/scatter-add | solution.py:108
  137.5 5.1 %all-to-all-start.2 = ((bf16[128,32,128]{0,2,1:T(8,128)(2,1)}), bf16[128,32,128]{0,2,1:T(8,128)(2,1)}, u32[]{:S(2)}, u32[]{:S(2)}) async-start(bf16[128,32,128]{0,2,1:T(8,128)(2,1)} %bitcast.160), calls=%async_computation.2 | async-start | bytes 2097152 | tf_op jit(solution)/shard_map/all_to_all | solution.py:79
  142.8 27.5 %all-to-all-done.2 = bf16[128,32,128]{0,2,1:T(8,128)(2,1)} async-done(((bf16[128,32,128]{0,2,1:T(8,128)(2,1)}), bf16[128,32,128]{0,2,1:T(8,128)(2,1)}, u32[]{:S(2)}, u32[]{:S(2)}) %all-to-all-start.2) | async-done | bytes 1048608 | tf_op jit(solution)/shard_map/all_to_all | solution.py:79
  170.3 23.1 %scatter_custom_fusion.1 = f32[128,1024]{0,1:T(8,128)S(1)} fusion(f32[128,1024]{0,1:T(8,128)S(1)} %slice.66, s32[4096]{0:T(1024)S(1)} %bitcast.173, bf16[128,4096]{0,1:T(8,128)(2,1)} %bitcast.44), kind=kCustom, calls=%fused_computation.22 | custom fusion | flops 1048576 | bytes 1572864 | tf_op jit(solution)/shard_map/scatter-add | solution.py:82
  198.1 12.1 %gather_fusion.3 = bf16[4096,128]{1,0:T(8,128)(2,1)S(1)} fusion(bf16[128,1024]{0,1:T(8,128)(2,1)S(1)} %fusion.25, s32[4096]{0:T(1024)S(1)} %fusion.49), kind=kCustom, calls=%fused_computation.2.clone | custom fusion | bytes 2113536 | tf_op jit(solution)/shard_map/jit(_take)/gather | solution.py:74
  213.1 5.1 %all-to-all-start.3 = ((bf16[128,32,128]{0,2,1:T(8,128)(2,1)}), bf16[128,32,128]{0,2,1:T(8,128)(2,1)S(1)}, u32[]{:S(2)}, u32[]{:S(2)}) async-start(bf16[128,32,128]{0,2,1:T(8,128)(2,1)} %bitcast.158), calls=%async_computation.3 | async-start | bytes 2097152 | tf_op jit(solution)/shard_map/all_to_all | solution.py:75
  220.2 25.7 %all-to-all-done.3 = bf16[128,32,128]{0,2,1:T(8,128)(2,1)S(1)} async-done(((bf16[128,32,128]{0,2,1:T(8,128)(2,1)}), bf16[128,32,128]{0,2,1:T(8,128)(2,1)S(1)}, u32[]{:S(2)}, u32[]{:S(2)}) %all-to-all-start.3) | async-done | bytes 1048608 | tf_op jit(solution)/shard_map/all_to_all | solution.py:75
  246.0 15.0 %gather_fusion.4 = bf16[4096,128]{1,0:T(8,128)(2,1)} fusion(bf16[128,5120]{0,1:T(8,128)(2,1)S(1)} %pad_maximum_fusion.2, s32[4096]{0:T(1024)S(1)} %get-tuple-element.41), kind=kCustom, calls=%fused_computation.4.clone | custom fusion | bytes 2113536 | tf_op jit(solution)/shard_map/jit(_take)/gather | solution.py:142
  273.7 23.3 %scatter_custom_fusion.2 = f32[128,5120]{0,1:T(8,128)S(1)} fusion(s32[4096]{0:T(1024)} %bitcast.175, f32[4096,128]{1,0:T(8,128)} %fusion.45, f32[]{:T(128)} %constant.27.clone.1), kind=kCustom, calls=%fused_computation.45 | custom fusion | flops 524288 | bytes 2621952 | tf_op jit(solution)/shard_map/scatter-add | solution.py:157
  297.0 3.0 fusion.43
  299.9 23.8 %scatter_fusion = f32[128,5120]{0,1:T(8,128)S(1)} fusion(f32[128,5120]{0,1:T(8,128)S(1)} %scatter_custom_fusion.2, s32[4096]{0:T(1024)S(1)} %bitcast.171, f32[4096,128]{1,0:T(8,128)} %fusion.43), kind=kCustom, calls=%fused_computation.8 | custom fusion | flops 524288 | bytes 6307840 | tf_op jit(solution)/shard_map/scatter-add | solution.py:159
  324.9 5.1 %all-to-all-start.4 = ((bf16[128,32,128]{0,2,1:T(8,128)(2,1)}), bf16[128,32,128]{0,2,1:T(8,128)(2,1)}, u32[]{:S(2)}, u32[]{:S(2)}) async-start(bf16[128,32,128]{0,2,1:T(8,128)(2,1)} %bitcast.159), calls=%async_computation.4 | async-start | bytes 2097152 | tf_op jit(solution)/shard_map/all_to_all | solution.py:79
  333.7 34.5 %all-to-all-done.4 = bf16[128,32,128]{0,2,1:T(8,128)(2,1)} async-done(((bf16[128,32,128]{0,2,1:T(8,128)(2,1)}), bf16[128,32,128]{0,2,1:T(8,128)(2,1)}, u32[]{:S(2)}, u32[]{:S(2)}) %all-to-all-start.4) | async-done | bytes 1048608 | tf_op jit(solution)/shard_map/all_to_all | solution.py:79
  368.2 23.0 %scatter_custom_fusion.4 = f32[128,1024]{0,1:T(8,128)S(1)} fusion(f32[128,1024]{0,1:T(8,128)S(1)} %copy.42, s32[4096]{0:T(1024)} %bitcast.174, bf16[128,4096]{0,1:T(8,128)(2,1)} %bitcast.46), kind=kCustom, calls=%fused_computation.20 | custom fusion | flops 1048576 | bytes 1572864 | tf_op jit(solution)/shard_map/scatter-add | solution.py:82
  392.2 24.8 %all-gather.3.cloned.1.call-done = bf16[32,1,115456]{2,1,0:T(2,128)(2,1)} async-done(((bf16[1,1,115456]{2,1,0:T(2,128)(2,1)}), bf16[32,1,115456]{2,1,0:T(2,128)(2,1)}) %all-gather.3.cloned.1.call-update) | async-done | bytes 7389200 | tf_op jit(solution)/shard_map/all_gather | solution.py:9
  417.0 20.8 %reduce_sum.152 = bf16[115456]{0:T(1024)(128)(2,1)S(1)} reduce(bf16[32,1,115456]{2,1,0:T(2,128)(2,1)} %all-gather.3.cloned.1.call-done, bf16[]{:T(256)} %constant.57.clone.1), dimensions={0,1}, to_apply=%region_19.22 | reduce | flops 3579136 | bytes 7620098 | tf_op jit(solution)/shard_map/reduce_sum | solution.py:10
  (176 shorter events, 44.4 us)
Async XLA Ops:
  7.2 101.9 %copy-start = (bf16[128,128]{1,0:T(8,128)(2,1)S(1)}, bf16[128,128]{1,0:T(8,128)(2,1)}, u32[]{:S(2)}) copy-start(bf16[128,128]{1,0:T(8,128)(2,1)} %param.29) | copy-start | bytes 98308
  7.2 21.2 %all-to-all-start = ((s32[32,1,128]{2,1,0:T(1,128)}), s32[32,1,128]{2,1,0:T(1,128)S(1)}, u32[]{:S(2)}, u32[]{:S(2)}) async-start(s32[32,1,128]{2,1,0:T(1,128)} %bitcast.172), calls=%async_computation | async-start | bytes 32768 | tf_op jit(solution)/shard_map/all_to_all | solution.py:69
  40.6 7.0 %copy-start.40 = (s32[32,2]{0,1:T(2,128)S(1)}, s32[32,2]{0,1:T(2,128)}, u32[]{:S(2)}) copy-start(s32[32,2]{0,1:T(2,128)} %param.24) | copy-start | bytes 772
  43.5 4.2 copy-start.10
  43.5 5.5 %copy-start.34 = (s32[32,2,128]{2,1,0:T(2,128)S(1)}, s32[32,2,128]{2,1,0:T(2,128)}, u32[]{:S(2)}) copy-start(s32[32,2,128]{2,1,0:T(2,128)} %param.25) | copy-start | bytes 98308
  43.5 31.6 %all-to-all-start.1 = ((bf16[128,32,128]{0,2,1:T(8,128)(2,1)}), bf16[128,32,128]{0,2,1:T(8,128)(2,1)S(1)}, u32[]{:S(2)}, u32[]{:S(2)}) async-start(bf16[128,32,128]{0,2,1:T(8,128)(2,1)} %bitcast.156), calls=%async_computation.1 | async-start | bytes 2097152 | tf_op jit(solution)/shard_map/all_to_all | solution.py:75
  49.1 55.4 %copy-start.30 = (pred[4096]{0:T(1024)(128)(4,1)}, pred[4096]{0:T(1024)(128)(4,1)S(1)}, u32[]{:S(2)}) copy-start(pred[4096]{0:T(1024)(128)(4,1)S(1)} %compare_and_fusion) | copy-start | bytes 12292
  49.8 63.4 %copy-start.26 = (s32[4096,1]{0,1:T(1,128)}, s32[4096,1]{0,1:T(1,128)S(1)}, u32[]{:S(2)}) copy-start(s32[4096,1]{0,1:T(1,128)S(1)} %get-tuple-element.26) | copy-start | bytes 49156
  102.4 4.4 copy-start.11
  102.4 4.4 copy-start.24
  102.4 4.4 copy-start.45
  104.6 4.5 %copy-start.13 = (bf16[128,4096]{0,1:T(8,128)(2,1)}, bf16[128,4096]{0,1:T(8,128)(2,1)S(1)}, u32[]{:S(2)}) copy-start(bf16[128,4096]{0,1:T(8,128)(2,1)S(1)} %select_bitcast_fusion.1) | copy-start | bytes 3145732
  137.5 32.7 %all-to-all-start.2 = ((bf16[128,32,128]{0,2,1:T(8,128)(2,1)}), bf16[128,32,128]{0,2,1:T(8,128)(2,1)}, u32[]{:S(2)}, u32[]{:S(2)}) async-start(bf16[128,32,128]{0,2,1:T(8,128)(2,1)} %bitcast.160), calls=%async_computation.2 | async-start | bytes 2097152 | tf_op jit(solution)/shard_map/all_to_all | solution.py:79
  142.7 50.8 %copy-start.46 = (f32[128]{0:T(128)S(1)}, f32[128]{0:T(128)}, u32[]{:S(2)}) copy-start(f32[128]{0:T(128)} %param.33) | copy-start | bytes 1540
  142.7 52.1 %copy-start.35 = (s32[4096,1]{0,1:T(1,128)}, s32[4096,1]{0,1:T(1,128)S(1)}, u32[]{:S(2)}) copy-start(s32[4096,1]{0,1:T(1,128)S(1)} %compare_select_fusion.1) | copy-start | bytes 49156
  197.9 21.0 %copy-start.8 = (bf16[128,1024]{0,1:T(8,128)(2,1)}, bf16[128,1024]{0,1:T(8,128)(2,1)S(1)}, u32[]{:S(2)}) copy-start(bf16[128,1024]{0,1:T(8,128)(2,1)S(1)} %get-tuple-element.39) | copy-start | bytes 786436
  213.1 5.8 %copy-start.23 = (bf16[128,1024]{0,1:T(8,128)(2,1)S(1)}, bf16[128,1024]{0,1:T(8,128)(2,1)}, u32[]{:S(2)}) copy-start(bf16[128,1024]{0,1:T(8,128)(2,1)} %copy-done.22) | copy-start | bytes 786436
  213.1 6.8 %copy-start.19 = (bf16[128,1024]{1,0:T(8,128)(2,1)S(1)}, bf16[128,1024]{1,0:T(8,128)(2,1)}, u32[]{:S(2)}) copy-start(bf16[128,1024]{1,0:T(8,128)(2,1)} %copy-done.18) | copy-start | bytes 786436
  213.1 32.8 %all-to-all-start.3 = ((bf16[128,32,128]{0,2,1:T(8,128)(2,1)}), bf16[128,32,128]{0,2,1:T(8,128)(2,1)S(1)}, u32[]{:S(2)}, u32[]{:S(2)}) async-start(bf16[128,32,128]{0,2,1:T(8,128)(2,1)} %bitcast.158), calls=%async_computation.3 | async-start | bytes 2097152 | tf_op jit(solution)/shard_map/all_to_all | solution.py:75
  218.2 198.8 %all-gather.3.cloned.1.call-start = ((), (), s32[]{:S(2)}) async-start(), calls=%async_computation.5 | async-start | bytes 15240192 | tf_op jit(solution)/shard_map/all_gather | solution.py:9
  246.0 16.7 %copy-start.31 = (pred[4096]{0:T(1024)(128)(4,1)S(1)}, pred[4096]{0:T(1024)(128)(4,1)}, u32[]{:S(2)}) copy-start(pred[4096]{0:T(1024)(128)(4,1)} %copy-done.30) | copy-start | bytes 12292
  246.0 16.7 %copy-start.37 = (f32[128]{0:T(128)S(1)}, f32[128]{0:T(128)}, u32[]{:S(2)}) copy-start(f32[128]{0:T(128)} %param.30) | copy-start | bytes 1540
  273.7 23.3 %copy-start.25 = (bf16[128,384]{1,0:T(8,128)(2,1)S(1)}, bf16[128,384]{1,0:T(8,128)(2,1)}, u32[]{:S(2)}) copy-start(bf16[128,384]{1,0:T(8,128)(2,1)} %param.27) | copy-start | bytes 294916
  324.9 43.4 %all-to-all-start.4 = ((bf16[128,32,128]{0,2,1:T(8,128)(2,1)}), bf16[128,32,128]{0,2,1:T(8,128)(2,1)}, u32[]{:S(2)}, u32[]{:S(2)}) async-start(bf16[128,32,128]{0,2,1:T(8,128)(2,1)} %bitcast.159), calls=%async_computation.4 | async-start | bytes 2097152 | tf_op jit(solution)/shard_map/all_to_all | solution.py:79
  (31 other events, 51.9 us)
Sparse Core Ops, SparseCore 0:
  271.3 145.6 all-gather.2
